TPU v7x, 32 devices: a whole 2x2x4 slice. The times are simulated.
32 devices in a mesh: stn: 16 (over z, y, core), pol: 2 (over x).
Axes of the slice: x: 2, y: 2, z: 4, core: 2. Of those that a mesh axis runs over, the one named last changes fastest.
Arguments:
- voltages: bfloat16 [64, 2, 2, 132992], P('stn', 'pol'), may hold values from -6 to 6, as said below
- delay_table: int32 [64], P('stn'), may hold values from 0 to 128
- channel_map: int32 [256], replicated, may hold values from 0 to 255, each once
- row_assign: int32 [32], replicated, may hold values from 0 to 31, each once
Outputs:
- bandpass: float32 [256, 128], P(('stn', 'pol'))
- lags: bfloat16 [32, 2, 256, 4, 128], P(('stn', 'pol'))
- delays: float32 [32, 4, 128], P(('stn', 'pol'))
Inputs may be any that keep to these rules, and one draw needn't show every extreme that they name: `voltages`: A station's two polarizations and its real and imaginary parts are noisy copies of common signals with station-dependent time shifts. `channel_map`: each channel appears in exactly one slot. `row_assign`: each row block appears in exactly one slot.
All inputs are finite; a program needn't handle non-finite values.
Results may differ from a plain program's by a relative error of at most 0.0059.
Values may be sent and summed in bfloat16 or wider, within the bound.
A program may use at most 128 MiB of HBM per device.

v0:
```python
import math
import jax
import jax.numpy as jnp
from jax import lax
from jax.sharding import PartitionSpec as P

CHANNELS = 256
TAPS = 8
SPECTRA = 512


def prototype():
    tap_total = TAPS * CHANNELS
    sample_index = jnp.arange(tap_total, dtype=jnp.float32)
    taper_values = 0.5 - 0.5 * jnp.cos(2.0 * math.pi * (sample_index + 0.5) / tap_total)
    offset = (sample_index - (tap_total - 1) / 2.0) / CHANNELS
    values = jnp.sin(math.pi * offset) / (math.pi * offset) * taper_values
    values = values * jnp.sqrt(CHANNELS / jnp.sum(values * values))
    return values.reshape(TAPS, CHANNELS)


def phase_parts(channels):
    cell_index = jnp.arange(CHANNELS, dtype=jnp.int32)
    phase_turns = channels[:, None] * cell_index[None, :] % CHANNELS
    phase_angle = phase_turns.astype(jnp.float32) * (2.0 * math.pi / CHANNELS)
    scale_factor = 1.0 / math.sqrt(CHANNELS)
    return (jnp.cos(phase_angle) * scale_factor, jnp.sin(phase_angle) * scale_factor)


def channel_table(channels):
    cosine, sine_part = phase_parts(channels)
    forward = jnp.stack([jnp.stack([cosine, sine_part], 1), jnp.stack([-sine_part, cosine], 1)], 0)
    return forward.astype(jnp.bfloat16)


def lag_table(channels):
    cosine, sine_part = phase_parts(channels)
    cosine = cosine.T
    sine_part = sine_part.T
    backward = jnp.stack([jnp.stack([cosine, -sine_part], 2), jnp.stack([sine_part, cosine], 2)], 0)
    return backward.astype(jnp.bfloat16)


def filter_bank(segment, window):
    framed = segment.reshape(segment.shape[:-1] + (SPECTRA + TAPS - 1, CHANNELS))
    total = jnp.zeros(segment.shape[:-1] + (SPECTRA, CHANNELS), jnp.float32)
    for tap_index in range(TAPS):
        total = (
            total
            + framed[..., tap_index : tap_index + SPECTRA, :].astype(jnp.float32)
            * window[tap_index]
        )
    return total.astype(jnp.bfloat16)


def per_device(voltages, delay_table, channel_map, row_assign):
    stn_count = lax.axis_size("stn")
    pol_count = lax.axis_size("pol")
    owner_count = stn_count * pol_count
    local_channels = CHANNELS // owner_count
    span = (SPECTRA + TAPS - 1) * CHANNELS
    window = prototype()
    position = jnp.arange(CHANNELS, dtype=jnp.int32)
    forward = channel_table(jnp.take(channel_map, position))

    def cut_segment(station_volts, start_sample):
        return lax.dynamic_slice_in_dim(station_volts, start_sample, span, 2)

    segment = jax.vmap(cut_segment)(voltages, delay_table)
    filtered = filter_bank(segment, window)
    spectra = jnp.einsum(
        "qkpc,tapsc->taqks", forward, filtered, preferred_element_type=jnp.float32
    ).astype(jnp.bfloat16)
    turned = lax.all_to_all(
        lax.all_to_all(spectra, "stn", split_axis=3, concat_axis=0, tiled=True),
        "pol",
        split_axis=3,
        concat_axis=1,
        tiled=True,
    )
    input_count = 2 * turned.shape[0]

    def correlate(channel_slot):
        channel_block = lax.dynamic_index_in_dim(turned, channel_slot, 3, keepdims=False)
        real_part = channel_block[:, :, 0].reshape(input_count, SPECTRA)
        imag_part = channel_block[:, :, 1].reshape(input_count, SPECTRA)
        stacked = jnp.concatenate([real_part, imag_part], 1)
        rotated = jnp.concatenate([-imag_part, real_part], 1)
        partner = jnp.concatenate([stacked, rotated], 0)
        product = (
            lax.dot_general(
                stacked, partner, (((1,), (1,)), ((), ())), preferred_element_type=jnp.float32
            )
            / SPECTRA
        )
        vis_real = product[:, :input_count]
        vis_imag = product[:, input_count:]
        return (jnp.stack([vis_real, vis_imag]).astype(jnp.bfloat16), jnp.diagonal(vis_real))

    visibility, bandpass = lax.map(correlate, jnp.arange(local_channels, dtype=jnp.int32))
    row_block = input_count // owner_count
    blocked = visibility.reshape(local_channels, 2, owner_count, row_block, input_count)
    block_index = jnp.arange(owner_count, dtype=jnp.int32)
    arranged = jnp.take(blocked, jnp.take(row_assign, block_index), axis=2)
    arranged = arranged.reshape(1, 1, local_channels, 2, input_count, input_count)
    regrouped = lax.all_to_all(
        lax.all_to_all(arranged, "stn", split_axis=4, concat_axis=0, tiled=True),
        "pol",
        split_axis=4,
        concat_axis=1,
        tiled=True,
    )
    gathered = regrouped.reshape(CHANNELS, 2, row_block * input_count)
    backward = lag_table(channel_map)
    lag = jnp.einsum("qlkp,kpm->qlm", backward, gathered, preferred_element_type=jnp.float32)
    power = lag[0] * lag[0] + lag[1] * lag[1]
    lag_position = jnp.where(position < CHANNELS // 2, position, position - CHANNELS).astype(
        jnp.float32
    ) / (CHANNELS // 2)
    delay = jnp.sum(power * lag_position[:, None], 0) / (jnp.sum(power, 0) + 1e-06)
    lags = lag.astype(jnp.bfloat16).reshape(1, 2, CHANNELS, row_block, input_count)
    delays = delay.reshape(1, row_block, input_count)
    return (bandpass, lags, delays)


def solution(mesh):
    in_specs = (P("stn", "pol", None, None), P("stn"), P(), P())
    out_specs = (
        P(("stn", "pol"), None),
        P(("stn", "pol"), None, None, None, None),
        P(("stn", "pol"), None, None),
    )
    return jax.shard_map(
        per_device, mesh=mesh, in_specs=in_specs, out_specs=out_specs, check_vma=False
    )
```

profile of v0, /device:TPU:0, one launch (start us, length us, event | category | flops | bytes accessed | tf_op | source)
XLA Modules:
  0.0 214.2 jit_solution(16711043971199102568)
XLA Ops:
  0.6 0.7 multiply_reduce_fusion
  1.3 2.0 gather_fusion.1
  3.3 1.3 fusion.30
  5.5 0.7 fusion.42
  6.2 17.1 %while.14 = (s32[]{:T(128)}, bf16[4,1,2,132992]{3,2,1,0:T(2,128)(2,1)}, s32[4,4]{1,0:T(4,128)S(1)}, bf16[4,1,2,132864]{3,2,1,0:T(2,128)(2,1)}, s32[]{:T(128)}) while((s32[]{:T(128)}, bf16[4,1,2,132992]{3,2,1,0:T(2,128)(2,1)}, s32[4,4]{1,0:T(4,128)S(1)}, bf16[4,1,2,132864]{3,2,1,0:T(2,128)(2,1)}, s32[]{:T(128)}) %tuple.66), condition=%wide.while_cond, body=%wide.while_body.sunk | while | flops 2 | bytes 1064561 | solution.py:67
  6.2 0.6 fusion.62
  6.8 3.7 %dynamic-slice_dynamic-update-slice_fusion.2 = bf16[4,1,2,132864]{3,2,1,0:T(2,128)(2,1)} fusion(bf16[4,1,2,132864]{3,2,1,0:T(2,128)(2,1)} %get-tuple-element.198, s32[]{:T(128)} %get-tuple-element.195, bf16[4,1,2,132992]{3,2,1,0:T(2,128)(2,1)} %get-tuple-element.201, s32[]{:T(128)} %bitcast.103, s32[]{:T(128)} %bitcast.104), kind=kLoop, calls=%fused_computation.4.clone.1 | loop fusion | bytes 1064448 | tf_op jit(solution)/shard_map/vmap()/gather
  10.5 0.6 fusion.62
  11.1 3.7 %dynamic-slice_dynamic-update-slice_fusion.2 = bf16[4,1,2,132864]{3,2,1,0:T(2,128)(2,1)} fusion(bf16[4,1,2,132864]{3,2,1,0:T(2,128)(2,1)} %get-tuple-element.198, s32[]{:T(128)} %get-tuple-element.195, bf16[4,1,2,132992]{3,2,1,0:T(2,128)(2,1)} %get-tuple-element.201, s32[]{:T(128)} %bitcast.103, s32[]{:T(128)} %bitcast.104), kind=kLoop, calls=%fused_computation.4.clone.1 | loop fusion | bytes 1064448 | tf_op jit(solution)/shard_map/vmap()/gather
  15.4 3.7 %dynamic-slice_dynamic-update-slice_fusion.2 = bf16[4,1,2,132864]{3,2,1,0:T(2,128)(2,1)} fusion(bf16[4,1,2,132864]{3,2,1,0:T(2,128)(2,1)} %get-tuple-element.198, s32[]{:T(128)} %get-tuple-element.195, bf16[4,1,2,132992]{3,2,1,0:T(2,128)(2,1)} %get-tuple-element.201, s32[]{:T(128)} %bitcast.103, s32[]{:T(128)} %bitcast.104), kind=kLoop, calls=%fused_computation.4.clone.1 | loop fusion | bytes 1064448 | tf_op jit(solution)/shard_map/vmap()/gather
  19.6 3.7 %dynamic-slice_dynamic-update-slice_fusion.2 = bf16[4,1,2,132864]{3,2,1,0:T(2,128)(2,1)} fusion(bf16[4,1,2,132864]{3,2,1,0:T(2,128)(2,1)} %get-tuple-element.198, s32[]{:T(128)} %get-tuple-element.195, bf16[4,1,2,132992]{3,2,1,0:T(2,128)(2,1)} %get-tuple-element.201, s32[]{:T(128)} %bitcast.103, s32[]{:T(128)} %bitcast.104), kind=kLoop, calls=%fused_computation.4.clone.1 | loop fusion | bytes 1064448 | tf_op jit(solution)/shard_map/vmap()/gather
  23.3 4.8 %reshape.434 = bf16[4,1,2,519,256]{4,3,2,0,1:T(8,128)(2,1)S(1)} reshape(bf16[4,1,2,132864]{3,2,1,0:T(2,128)(2,1)} %get-tuple-element.40) | data formatting | bytes 4251648 | tf_op jit(solution)/shard_map/reshape | solution.py:45
  28.2 5.6 %fusion.8 = bf16[4,1,2,256,512]{3,4,2,0,1:T(8,128)(2,1)} fusion(f32[256]{0:T(256)S(1)} %get-tuple-element.103, bf16[4,1,2,519,256]{4,3,2,0,1:T(8,128)(2,1)S(1)} %reshape.434, f32[256]{0:T(256)S(1)} %get-tuple-element.104, f32[256]{0:T(256)S(1)} %get-tuple-element.105, f32[256]{0:T(256)S(1)} %get-tuple-element.106, f32[256]{0:T(256)S(1)} %get-tuple-element.107, ...), kind=kOutput, calls=%fused_computation.25 | convolution fusion | flops 1101004800 | bytes 19406848 | tf_op jit(solution)/shard_map/qkpc,tapsc->taqks/dot_general | solution.py:71
  33.8 4.9 %copy.25 = bf16[4,1,2,256,512]{4,2,0,1,3:T(2,128)(2,1)S(1)} copy(bf16[4,1,2,256,512]{3,4,2,0,1:T(8,128)(2,1)} %fusion.8) | data formatting | bytes 4194304 | tf_op jit(solution)/shard_map/convert_element_type | solution.py:73
  38.7 54.4 %all_to_all.69 = bf16[4,1,2,256,512]{4,2,0,1,3:T(2,128)(2,1)S(1)} all-to-all(bf16[4,1,2,256,512]{4,2,0,1,3:T(2,128)(2,1)S(1)} %copy.25), channel_id=1, replica_groups=mesh['stn'=16,'pol'=2] {'stn'}, dimensions={3} | all-to-all | bytes 4194304 | tf_op jit(solution)/shard_map/all_to_all | solution.py:75
  93.1 0.7 copy.26
  94.1 3.5 %copy.28 = bf16[64,1,2,16,512]{4,2,0,1,3:T(2,128)(2,1)} copy(bf16[64,1,2,16,512]{4,3,2,0,1:T(8,128)(2,1)S(1)} %bitcast.106) | data formatting | bytes 4194304 | tf_op jit(solution)/shard_map/all_to_all | solution.py:75
  97.6 3.9 %all-to-all-start.1 = ((bf16[64,1,2,16,512]{4,2,0,1,3:T(2,128)(2,1)}), bf16[64,1,2,16,512]{4,2,0,1,3:T(2,128)(2,1)S(1)}, u32[]{:S(2)}, u32[]{:S(2)}) async-start(bf16[64,1,2,16,512]{4,2,0,1,3:T(2,128)(2,1)} %copy.28), calls=%async_computation.1 | async-start | bytes 4194304 | tf_op jit(solution)/shard_map/all_to_all | solution.py:74
  101.6 0.7 gather_fusion.2
  102.5 25.1 %all-to-all-done.1 = bf16[64,1,2,16,512]{4,2,0,1,3:T(2,128)(2,1)S(1)} async-done(((bf16[64,1,2,16,512]{4,2,0,1,3:T(2,128)(2,1)}), bf16[64,1,2,16,512]{4,2,0,1,3:T(2,128)(2,1)S(1)}, u32[]{:S(2)}, u32[]{:S(2)}) %all-to-all-start.1) | async-done | bytes 2097184 | tf_op jit(solution)/shard_map/all_to_all | solution.py:74
  127.6 2.2 %copy.41 = bf16[64,1,2,16,512]{4,3,2,0,1:T(8,128)(2,1)S(1)} copy(bf16[64,1,2,16,512]{4,2,0,1,3:T(2,128)(2,1)S(1)} %all-to-all-done.1) | data formatting | bytes 4194304 | tf_op jit(solution)/shard_map/all_to_all | solution.py:74
  129.8 1.2 copy.30
  131.0 47.9 %while.13 = (s32[]{:T(128)}, bf16[8,2,128,128]{3,2,1,0:T(8,128)(2,1)S(1)}, f32[8,128]{1,0:T(8,128)}, s32[8]{0:T(128)S(1)}, bf16[64,2,2,8,512]{4,0,3,2,1:T(8,128)(2,1)S(1)}, /*index=5*/s32[]{:T(128)}, s32[]{:T(128)}, s32[]{:T(128)}) while((s32[]{:T(128)}, bf16[8,2,128,128]{3,2,1,0:T(8,128)(2,1)S(1)}, f32[8,128]{1,0:T(8,128)}, s32[8]{0:T(128)S(1)}, ...), condition=%wide.region_2.3_spmd, body=%wide.region_1.2_spmd.sunk | while | flops 69042688 | bytes 3804815 | solution.py:100
  131.0 0.6 dynamic_slice.12
  134.5 1.2 gather_fusion
  135.7 1.3 dynamic_update_slice.12
  140.4 1.2 gather_fusion
  141.7 1.3 dynamic_update_slice.12
  146.4 1.2 gather_fusion
  147.7 1.3 dynamic_update_slice.12
  152.4 1.2 gather_fusion
  153.7 1.3 dynamic_update_slice.12
  158.4 1.2 gather_fusion
  159.7 1.3 dynamic_update_slice.12
  164.4 1.2 gather_fusion
  165.7 1.3 dynamic_update_slice.12
  170.4 1.2 gather_fusion
  171.6 1.3 dynamic_update_slice.12
  176.4 1.2 gather_fusion
  177.6 1.3 dynamic_update_slice.12
  179.3 0.6 gather_fusion.3
  180.3 18.6 %all_to_all.70 = bf16[1,1,8,2,128,128]{5,2,3,1,0,4:T(8,128)(2,1)S(1)} all-to-all(bf16[1,1,8,2,128,128]{5,2,3,1,0,4:T(8,128)(2,1)S(1)} %copy.33), channel_id=1, replica_groups=mesh['stn'=16,'pol'=2] {'stn'}, dimensions={4} | all-to-all | bytes 1048576 | tf_op jit(solution)/shard_map/all_to_all | solution.py:107
  198.9 0.9 copy.42
  199.9 3.5 %all-to-all-start.3 = ((bf16[16,1,8,2,8,128]{5,2,0,3,1,4:T(8,128)(2,1)}), bf16[16,1,8,2,8,128]{5,2,0,3,1,4:T(8,128)(2,1)S(1)}, u32[]{:S(2)}, u32[]{:S(2)}) async-start(bf16[16,1,8,2,8,128]{5,2,0,3,1,4:T(8,128)(2,1)} %bitcast.88), calls=%async_computation.3 | async-start | bytes 1048576 | tf_op jit(solution)/shard_map/all_to_all | solution.py:106
  203.4 1.2 negate_convert_fusion
  204.6 7.3 %all-to-all-done.3 = bf16[16,1,8,2,8,128]{5,2,0,3,1,4:T(8,128)(2,1)S(1)} async-done(((bf16[16,1,8,2,8,128]{5,2,0,3,1,4:T(8,128)(2,1)}), bf16[16,1,8,2,8,128]{5,2,0,3,1,4:T(8,128)(2,1)S(1)}, u32[]{:S(2)}, u32[]{:S(2)}) %all-to-all-start.3) | async-done | bytes 524320 | tf_op jit(solution)/shard_map/all_to_all | solution.py:106
  212.7 0.9 reshape.438
  213.6 0.6 fusion.39
  (152 shorter events, 14.1 us)
Async XLA Ops:
  0.6 101.0 %copy-start = (s32[32]{0:T(128)S(1)}, s32[32]{0:T(128)}, u32[]{:S(2)}) copy-start(s32[32]{0:T(128)} %param.9) | copy-start | bytes 388
  97.6 30.0 %all-to-all-start.1 = ((bf16[64,1,2,16,512]{4,2,0,1,3:T(2,128)(2,1)}), bf16[64,1,2,16,512]{4,2,0,1,3:T(2,128)(2,1)S(1)}, u32[]{:S(2)}, u32[]{:S(2)}) async-start(bf16[64,1,2,16,512]{4,2,0,1,3:T(2,128)(2,1)} %copy.28), calls=%async_computation.1 | async-start | bytes 4194304 | tf_op jit(solution)/shard_map/all_to_all | solution.py:74
  180.2 23.2 %copy-start.1 = (s32[256]{0:T(256)S(1)}, s32[256]{0:T(256)}, u32[]{:S(2)}) copy-start(s32[256]{0:T(256)} %param.8) | copy-start | bytes 3076
  199.9 12.0 %all-to-all-start.3 = ((bf16[16,1,8,2,8,128]{5,2,0,3,1,4:T(8,128)(2,1)}), bf16[16,1,8,2,8,128]{5,2,0,3,1,4:T(8,128)(2,1)S(1)}, u32[]{:S(2)}, u32[]{:S(2)}) async-start(bf16[16,1,8,2,8,128]{5,2,0,3,1,4:T(8,128)(2,1)} %bitcast.88), calls=%async_computation.3 | async-start | bytes 1048576 | tf_op jit(solution)/shard_map/all_to_all | solution.py:106
where the time goes:
time: 215 us; the launch traced here: 214 us
  blocking collectives  73 us (34%)
  local copies, waits for them, and re-layouts  69.6 us (32%)
  waiting for transfers between devices  32.4 us (15%)
  loops' own time  16.3 us (8%)
  matrix products  8.48 us (4%)
  starting transfers between devices  7.43 us (3%)
  other arithmetic  5.45 us (3%)
    all_to_all x1, blocking collectives, per_device(): lax.all_to_all(spectra, 'stn', split_axis=3, concat_axis=0, tiled=True)  54.4 us
    all_to_all x1, waiting for transfers between devices, per_device(): lax.all_to_all(lax.all_to_all(spectra, 'stn', split_axis=3, concat_axis=0...  25.1 us
    all_to_all x1, blocking collectives, per_device(): lax.all_to_all(arranged, 'stn', split_axis=4, concat_axis=0, tiled=True)  18.6 us
    gather x12, local copies, waits for them, and re-layouts  17.1 us
    another operation x1, loops' own time, per_device(): lax.map(correlate, jnp.arange(local_channels, dtype=jnp.int32))  16.3 us
    dynamic_update_slice x8, local copies, waits for them, and re-layouts, per_device(): lax.map(correlate, jnp.arange(local_channels, dtype=jnp.int32))  10.4 us
    gather x8, local copies, waits for them, and re-layouts, correlate(): jnp.diagonal(vis_real)  9.96 us
    all_to_all x1, waiting for transfers between devices, per_device(): lax.all_to_all(lax.all_to_all(arranged, 'stn', split_axis=4, concat_axis=...  7.31 us
  transfers between devices with their start and end apart: 2, of which 2 were waited for; matrix products, arithmetic and copies ran while one was open for 1% of the time, Pallas kernels for 0%

commit v1 on v0

--- a/solution.py
+++ b/solution.py
@@ -103,12 +103,29 @@
     block_index = jnp.arange(owner_count, dtype=jnp.int32)
     arranged = jnp.take(blocked, jnp.take(row_assign, block_index), axis=2)
     arranged = arranged.reshape(1, 1, local_channels, 2, input_count, input_count)
+
+    def _spread_results(axis_tag, x_in):
+        w1 = jax.lax.psum(1, axis_name=axis_tag)
+        t1 = jax.lax.axis_index(axis_tag)
+        tmp, part_now = (w1, t1)
+        found_now = x_in.shape[4] // tmp
+        z_new = list(x_in.shape)
+        z_new[4] = found_now
+        piece_out = z_new[0]
+        z_new[0] = piece_out * tmp
+        item_now = jnp.zeros(z_new, x_in.dtype)
+        for t in [*range(tmp)]:
+            known = lax.dynamic_slice_in_dim(x_in, (part_now ^ t) * found_now, found_now, axis=4)
+            if t:
+                r2 = tuple(((s, s ^ t) for s in range(tmp)))
+                known = jax.lax.ppermute(known, axis_tag, r2)
+            item_now = lax.dynamic_update_slice_in_dim(
+                item_now, known, (part_now ^ t) * piece_out, axis=0
+            )
+        return item_now
+
     regrouped = lax.all_to_all(
-        lax.all_to_all(arranged, "stn", split_axis=4, concat_axis=0, tiled=True),
-        "pol",
-        split_axis=4,
-        concat_axis=1,
-        tiled=True,
+        _spread_results("stn", arranged), "pol", split_axis=4, concat_axis=1, tiled=True
     )
     gathered = regrouped.reshape(CHANNELS, 2, row_block * input_count)
     backward = lag_table(channel_map)

time: 215 us -> 229 us (1.065)
  starting transfers between devices: 7.43 us -> 27.9 us
  blocking collectives: 73 us -> 54.4 us
  local copies, waits for them, and re-layouts: 69.6 us -> 79.5 us
    ppermute x0 -> x15, starting transfers between devices: none -> 20.5 us  [_spread_results(): known = jax.lax.ppermute(known, axis_tag, r2)]
    all_to_all x1 -> x0, blocking collectives: 18.6 us -> none  [per_device(): lax.all_to_all(arranged, 'stn', split_axis=4, concat_axis=0, tiled=True)]
    dynamic_update_slice x0 -> x16, local copies, waits for them, and re-layouts: none -> 9.92 us  [_spread_results(): lax.dynamic_update_slice_in_dim(item_now, known, (part_now ^ t) * piece_o...]
  transfers between devices with their start and end apart: 2 -> 17, of which waited for: 2 -> 3; matrix products, arithmetic and copies ran while one was open for 1% -> 5% of each run, Pallas kernels for 0% -> 0%
where the time goes in v1:
time: 229 us; the launch traced here: 228 us
  local copies, waits for them, and re-layouts  79.5 us (35%)
  blocking collectives  54.4 us (24%)
  waiting for transfers between devices  33.7 us (15%)
  starting transfers between devices  27.9 us (12%)
  loops' own time  16.3 us (7%)
  matrix products  8.44 us (4%)
  other arithmetic  5.47 us (2%)
    all_to_all x1, blocking collectives, per_device(): lax.all_to_all(spectra, 'stn', split_axis=3, concat_axis=0, tiled=True)  54.4 us
    all_to_all x1, waiting for transfers between devices, per_device(): lax.all_to_all(lax.all_to_all(spectra, 'stn', split_axis=3, concat_axis=0...  24.7 us
    ppermute x15, starting transfers between devices, _spread_results(): known = jax.lax.ppermute(known, axis_tag, r2)  20.5 us
    gather x12, local copies, waits for them, and re-layouts  17.1 us
    another operation x1, loops' own time, per_device(): lax.map(correlate, jnp.arange(local_channels, dtype=jnp.int32))  16.3 us
    dynamic_update_slice x8, local copies, waits for them, and re-layouts, per_device(): lax.map(correlate, jnp.arange(local_channels, dtype=jnp.int32))  10.4 us
    gather x8, local copies, waits for them, and re-layouts, correlate(): jnp.diagonal(vis_real)  9.96 us
    dynamic_update_slice x16, local copies, waits for them, and re-layouts, _spread_results(): lax.dynamic_update_slice_in_dim(item_now, known, (part_now ^ t) * piece_o...  9.92 us
  transfers between devices with their start and end apart: 17, of which 3 were waited for; matrix products, arithmetic and copies ran while one was open for 5% of the time, Pallas kernels for 0%

profile of v1, /device:TPU:0, one launch (start us, length us, event | category | flops | bytes accessed | tf_op | source)
XLA Modules:
  0.0 227.7 jit_solution(1248690887181721612)
XLA Ops:
  1.3 2.0 gather_fusion.1
  3.3 1.3 fusion.30
  6.2 17.1 %while.14 = (s32[]{:T(128)}, bf16[4,1,2,132992]{3,2,1,0:T(2,128)(2,1)}, s32[4,4]{1,0:T(4,128)S(1)}, bf16[4,1,2,132864]{3,2,1,0:T(2,128)(2,1)}, s32[]{:T(128)}) while((s32[]{:T(128)}, bf16[4,1,2,132992]{3,2,1,0:T(2,128)(2,1)}, s32[4,4]{1,0:T(4,128)S(1)}, bf16[4,1,2,132864]{3,2,1,0:T(2,128)(2,1)}, s32[]{:T(128)}) %tuple.81), condition=%wide.while_cond, body=%wide.while_body.sunk | while | flops 2 | bytes 1064561 | solution.py:67
  6.8 3.7 %dynamic-slice_dynamic-update-slice_fusion.2 = bf16[4,1,2,132864]{3,2,1,0:T(2,128)(2,1)} fusion(bf16[4,1,2,132864]{3,2,1,0:T(2,128)(2,1)} %get-tuple-element.214, s32[]{:T(128)} %get-tuple-element.211, bf16[4,1,2,132992]{3,2,1,0:T(2,128)(2,1)} %get-tuple-element.217, s32[]{:T(128)} %bitcast.97, s32[]{:T(128)} %bitcast.98), kind=kLoop, calls=%fused_computation.4.clone.1 | loop fusion | bytes 1064448 | tf_op jit(solution)/shard_map/vmap()/gather
  11.1 3.7 %dynamic-slice_dynamic-update-slice_fusion.2 = bf16[4,1,2,132864]{3,2,1,0:T(2,128)(2,1)} fusion(bf16[4,1,2,132864]{3,2,1,0:T(2,128)(2,1)} %get-tuple-element.214, s32[]{:T(128)} %get-tuple-element.211, bf16[4,1,2,132992]{3,2,1,0:T(2,128)(2,1)} %get-tuple-element.217, s32[]{:T(128)} %bitcast.97, s32[]{:T(128)} %bitcast.98), kind=kLoop, calls=%fused_computation.4.clone.1 | loop fusion | bytes 1064448 | tf_op jit(solution)/shard_map/vmap()/gather
  15.4 3.7 %dynamic-slice_dynamic-update-slice_fusion.2 = bf16[4,1,2,132864]{3,2,1,0:T(2,128)(2,1)} fusion(bf16[4,1,2,132864]{3,2,1,0:T(2,128)(2,1)} %get-tuple-element.214, s32[]{:T(128)} %get-tuple-element.211, bf16[4,1,2,132992]{3,2,1,0:T(2,128)(2,1)} %get-tuple-element.217, s32[]{:T(128)} %bitcast.97, s32[]{:T(128)} %bitcast.98), kind=kLoop, calls=%fused_computation.4.clone.1 | loop fusion | bytes 1064448 | tf_op jit(solution)/shard_map/vmap()/gather
  19.6 3.7 %dynamic-slice_dynamic-update-slice_fusion.2 = bf16[4,1,2,132864]{3,2,1,0:T(2,128)(2,1)} fusion(bf16[4,1,2,132864]{3,2,1,0:T(2,128)(2,1)} %get-tuple-element.214, s32[]{:T(128)} %get-tuple-element.211, bf16[4,1,2,132992]{3,2,1,0:T(2,128)(2,1)} %get-tuple-element.217, s32[]{:T(128)} %bitcast.97, s32[]{:T(128)} %bitcast.98), kind=kLoop, calls=%fused_computation.4.clone.1 | loop fusion | bytes 1064448 | tf_op jit(solution)/shard_map/vmap()/gather
  23.3 4.8 %reshape.434 = bf16[4,1,2,519,256]{4,3,2,0,1:T(8,128)(2,1)S(1)} reshape(bf16[4,1,2,132864]{3,2,1,0:T(2,128)(2,1)} %get-tuple-element.40) | data formatting | bytes 4251648 | tf_op jit(solution)/shard_map/reshape | solution.py:45
  28.2 5.5 %fusion.8 = bf16[4,1,2,256,512]{3,4,2,0,1:T(8,128)(2,1)} fusion(f32[256]{0:T(256)S(1)} %get-tuple-element.119, bf16[4,1,2,519,256]{4,3,2,0,1:T(8,128)(2,1)S(1)} %reshape.434, f32[256]{0:T(256)S(1)} %get-tuple-element.120, f32[256]{0:T(256)S(1)} %get-tuple-element.121, f32[256]{0:T(256)S(1)} %get-tuple-element.122, f32[256]{0:T(256)S(1)} %get-tuple-element.123, ...), kind=kOutput, calls=%fused_computation.25 | convolution fusion | flops 1101004800 | bytes 19406848 | tf_op jit(solution)/shard_map/qkpc,tapsc->taqks/dot_general | solution.py:71
  33.7 4.9 %copy.29 = bf16[4,1,2,256,512]{4,2,0,1,3:T(2,128)(2,1)S(1)} copy(bf16[4,1,2,256,512]{3,4,2,0,1:T(8,128)(2,1)} %fusion.8) | data formatting | bytes 4194304 | tf_op jit(solution)/shard_map/convert_element_type | solution.py:73
  38.7 54.4 %all_to_all.51 = bf16[4,1,2,256,512]{4,2,0,1,3:T(2,128)(2,1)S(1)} all-to-all(bf16[4,1,2,256,512]{4,2,0,1,3:T(2,128)(2,1)S(1)} %copy.29), channel_id=1, replica_groups=mesh['stn'=16,'pol'=2] {'stn'}, dimensions={3} | all-to-all | bytes 4194304 | tf_op jit(solution)/shard_map/all_to_all | solution.py:75
  94.0 3.5 %copy.32 = bf16[64,1,2,16,512]{4,2,0,1,3:T(2,128)(2,1)} copy(bf16[64,1,2,16,512]{4,3,2,0,1:T(8,128)(2,1)S(1)} %bitcast.100) | data formatting | bytes 4194304 | tf_op jit(solution)/shard_map/all_to_all | solution.py:75
  97.5 3.9 %all-to-all-start.1 = ((bf16[64,1,2,16,512]{4,2,0,1,3:T(2,128)(2,1)}), bf16[64,1,2,16,512]{4,2,0,1,3:T(2,128)(2,1)S(1)}, u32[]{:S(2)}, u32[]{:S(2)}) async-start(bf16[64,1,2,16,512]{4,2,0,1,3:T(2,128)(2,1)} %copy.32), calls=%async_computation.1 | async-start | bytes 4194304 | tf_op jit(solution)/shard_map/all_to_all | solution.py:74
  102.8 24.7 %all-to-all-done.1 = bf16[64,1,2,16,512]{4,2,0,1,3:T(2,128)(2,1)S(1)} async-done(((bf16[64,1,2,16,512]{4,2,0,1,3:T(2,128)(2,1)}), bf16[64,1,2,16,512]{4,2,0,1,3:T(2,128)(2,1)S(1)}, u32[]{:S(2)}, u32[]{:S(2)}) %all-to-all-start.1) | async-done | bytes 2097184 | tf_op jit(solution)/shard_map/all_to_all | solution.py:74
  127.5 2.2 copy.74
  129.7 1.2 copy.34
  130.9 48.0 %while.13 = (s32[]{:T(128)}, bf16[8,2,128,128]{3,2,1,0:T(8,128)(2,1)S(1)}, f32[8,128]{1,0:T(8,128)}, s32[8]{0:T(128)S(1)}, bf16[64,2,2,8,512]{4,0,3,2,1:T(8,128)(2,1)S(1)}, /*index=5*/s32[]{:T(128)}, s32[]{:T(128)}, s32[]{:T(128)}) while((s32[]{:T(128)}, bf16[8,2,128,128]{3,2,1,0:T(8,128)(2,1)S(1)}, f32[8,128]{1,0:T(8,128)}, s32[8]{0:T(128)S(1)}, ...), condition=%wide.region_2.3_spmd, body=%wide.region_1.2_spmd.sunk | while | flops 69042688 | bytes 3804815 | solution.py:100
  134.4 1.2 gather_fusion
  135.6 1.3 dynamic_update_slice.92
  140.4 1.2 gather_fusion
  141.6 1.3 dynamic_update_slice.92
  146.4 1.2 gather_fusion
  147.6 1.3 dynamic_update_slice.92
  152.4 1.2 gather_fusion
  153.6 1.3 dynamic_update_slice.92
  158.4 1.2 gather_fusion
  159.6 1.3 dynamic_update_slice.92
  164.4 1.2 gather_fusion
  165.6 1.3 dynamic_update_slice.92
  170.4 1.2 gather_fusion
  171.6 1.3 dynamic_update_slice.92
  176.4 1.2 gather_fusion
  177.6 1.3 dynamic_update_slice.92
  180.5 1.3 collective-permute-start.1
  182.3 1.7 collective-permute-start.3
  185.6 2.1 collective-permute-start.5
  189.4 1.6 collective-permute-start.7
  191.7 1.0 collective-permute-start.8
  193.3 2.0 collective-permute-start.9
  196.0 1.5 collective-permute-start.10
  198.1 2.0 collective-permute-start.11
  200.8 1.5 collective-permute-start.12
  202.9 3.1 %collective-permute-start.13 = (bf16[1,1,8,2,8,128]{5,2,4,3,1,0:T(8,128)(2,1)S(1)}, bf16[1,1,8,2,8,128]{5,2,4,3,1,0:T(8,128)(2,1)S(1)}, u32[]{:S(2)}, u32[]{:S(2)}) collective-permute-start(bf16[1,1,8,2,8,128]{5,2,4,3,1,0:T(8,128)(2,1)S(1)} %get-tuple-element.99), channel_id=1, source_target_pairs={{0,28},{2,30},{4,24},{6,26},{8,20},{10,22},{12,16},{14,18},{16,12}... | collective-permute-start | bytes 98312 | tf_op jit(solution)/shard_map/ppermute | solution.py:121
  206.7 1.3 collective-permute-start.14
  211.1 1.6 collective-permute-done.14
  213.4 3.5 %all-to-all-start.2 = ((bf16[16,1,8,2,8,128]{5,2,0,3,1,4:T(8,128)(2,1)}), bf16[16,1,8,2,8,128]{5,2,0,3,1,4:T(8,128)(2,1)S(1)}, u32[]{:S(2)}, u32[]{:S(2)}) async-start(bf16[16,1,8,2,8,128]{5,2,0,3,1,4:T(8,128)(2,1)} %copy_dynamic-update-slice_fusion), calls=%async_computation.2 | async-start | bytes 1048576 | tf_op jit(solution)/shard_map/all_to_all | solution.py:127
  216.9 1.2 negate_convert_fusion
  218.1 7.3 %all-to-all-done.2 = bf16[16,1,8,2,8,128]{5,2,0,3,1,4:T(8,128)(2,1)S(1)} async-done(((bf16[16,1,8,2,8,128]{5,2,0,3,1,4:T(8,128)(2,1)}), bf16[16,1,8,2,8,128]{5,2,0,3,1,4:T(8,128)(2,1)S(1)}, u32[]{:S(2)}, u32[]{:S(2)}) %all-to-all-start.2) | async-done | bytes 524320 | tf_op jit(solution)/shard_map/all_to_all | solution.py:127
  (197 shorter events, 33.0 us)
Async XLA Ops:
  0.6 101.1 %copy-start = (s32[32]{0:T(128)S(1)}, s32[32]{0:T(128)}, u32[]{:S(2)}) copy-start(s32[32]{0:T(128)} %param.9) | copy-start | bytes 388
  97.5 30.0 %all-to-all-start.1 = ((bf16[64,1,2,16,512]{4,2,0,1,3:T(2,128)(2,1)}), bf16[64,1,2,16,512]{4,2,0,1,3:T(2,128)(2,1)S(1)}, u32[]{:S(2)}, u32[]{:S(2)}) async-start(bf16[64,1,2,16,512]{4,2,0,1,3:T(2,128)(2,1)} %copy.32), calls=%async_computation.1 | async-start | bytes 4194304 | tf_op jit(solution)/shard_map/all_to_all | solution.py:74
  180.0 36.9 %copy-start.1 = (s32[256]{0:T(256)S(1)}, s32[256]{0:T(256)}, u32[]{:S(2)}) copy-start(s32[256]{0:T(256)} %param.8) | copy-start | bytes 3076
  180.4 5.2 %collective-permute-start = (bf16[1,1,8,2,8,128]{5,2,4,3,1,0:T(8,128)(2,1)S(1)}, bf16[1,1,8,2,8,128]{5,2,4,3,1,0:T(8,128)(2,1)S(1)}, u32[]{:S(2)}, u32[]{:S(2)}) collective-permute-start(bf16[1,1,8,2,8,128]{5,2,4,3,1,0:T(8,128)(2,1)S(1)} %get-tuple-element.112), channel_id=1, source_target_pairs={{0,2},{2,0},{4,6},{6,4},{8,10},{10,8},{12,14},{14,12},{16,18},{18,... | collective-permute-start | bytes 98312 | tf_op jit(solution)/shard_map/ppermute | solution.py:121
  180.5 7.7 %collective-permute-start.1 = (bf16[1,1,8,2,8,128]{5,2,4,3,1,0:T(8,128)(2,1)S(1)}, bf16[1,1,8,2,8,128]{5,2,4,3,1,0:T(8,128)(2,1)S(1)}, u32[]{:S(2)}, u32[]{:S(2)}) collective-permute-start(bf16[1,1,8,2,8,128]{5,2,4,3,1,0:T(8,128)(2,1)S(1)} %get-tuple-element.111), channel_id=1, source_target_pairs={{0,4},{2,6},{4,0},{6,2},{8,12},{10,14},{12,8},{14,10},{16,20},{18,... | collective-permute-start | bytes 98312 | tf_op jit(solution)/shard_map/ppermute | solution.py:121
  181.8 7.6 %collective-permute-start.2 = (bf16[1,1,8,2,8,128]{5,2,4,3,1,0:T(8,128)(2,1)S(1)}, bf16[1,1,8,2,8,128]{5,2,4,3,1,0:T(8,128)(2,1)S(1)}, u32[]{:S(2)}, u32[]{:S(2)}) collective-permute-start(bf16[1,1,8,2,8,128]{5,2,4,3,1,0:T(8,128)(2,1)S(1)} %get-tuple-element.110), channel_id=1, source_target_pairs={{0,6},{2,4},{4,2},{6,0},{8,14},{10,12},{12,10},{14,8},{16,22},{18,... | collective-permute-start | bytes 98312 | tf_op jit(solution)/shard_map/ppermute | solution.py:121
  182.3 9.4 %collective-permute-start.3 = (bf16[1,1,8,2,8,128]{5,2,4,3,1,0:T(8,128)(2,1)S(1)}, bf16[1,1,8,2,8,128]{5,2,4,3,1,0:T(8,128)(2,1)S(1)}, u32[]{:S(2)}, u32[]{:S(2)}) collective-permute-start(bf16[1,1,8,2,8,128]{5,2,4,3,1,0:T(8,128)(2,1)S(1)} %get-tuple-element.109), channel_id=1, source_target_pairs={{0,8},{2,10},{4,12},{6,14},{8,0},{10,2},{12,4},{14,6},{16,24},{18,... | collective-permute-start | bytes 98312 | tf_op jit(solution)/shard_map/ppermute | solution.py:121
  184.0 9.3 %collective-permute-start.4 = (bf16[1,1,8,2,8,128]{5,2,4,3,1,0:T(8,128)(2,1)S(1)}, bf16[1,1,8,2,8,128]{5,2,4,3,1,0:T(8,128)(2,1)S(1)}, u32[]{:S(2)}, u32[]{:S(2)}) collective-permute-start(bf16[1,1,8,2,8,128]{5,2,4,3,1,0:T(8,128)(2,1)S(1)} %get-tuple-element.108), channel_id=1, source_target_pairs={{0,10},{2,8},{4,14},{6,12},{8,2},{10,0},{12,6},{14,4},{16,26},{18,... | collective-permute-start | bytes 98312 | tf_op jit(solution)/shard_map/ppermute | solution.py:121
  185.6 10.4 %collective-permute-start.5 = (bf16[1,1,8,2,8,128]{5,2,4,3,1,0:T(8,128)(2,1)S(1)}, bf16[1,1,8,2,8,128]{5,2,4,3,1,0:T(8,128)(2,1)S(1)}, u32[]{:S(2)}, u32[]{:S(2)}) collective-permute-start(bf16[1,1,8,2,8,128]{5,2,4,3,1,0:T(8,128)(2,1)S(1)} %get-tuple-element.107), channel_id=1, source_target_pairs={{0,12},{2,14},{4,8},{6,10},{8,4},{10,6},{12,0},{14,2},{16,28},{18,... | collective-permute-start | bytes 98312 | tf_op jit(solution)/shard_map/ppermute | solution.py:121
  188.2 9.9 %collective-permute-start.6 = (bf16[1,1,8,2,8,128]{5,2,4,3,1,0:T(8,128)(2,1)S(1)}, bf16[1,1,8,2,8,128]{5,2,4,3,1,0:T(8,128)(2,1)S(1)}, u32[]{:S(2)}, u32[]{:S(2)}) collective-permute-start(bf16[1,1,8,2,8,128]{5,2,4,3,1,0:T(8,128)(2,1)S(1)} %get-tuple-element.106), channel_id=1, source_target_pairs={{0,14},{2,12},{4,10},{6,8},{8,6},{10,4},{12,2},{14,0},{16,30},{18,... | collective-permute-start | bytes 98312 | tf_op jit(solution)/shard_map/ppermute | solution.py:121
  189.4 11.3 %collective-permute-start.7 = (bf16[1,1,8,2,8,128]{5,2,4,3,1,0:T(8,128)(2,1)S(1)}, bf16[1,1,8,2,8,128]{5,2,4,3,1,0:T(8,128)(2,1)S(1)}, u32[]{:S(2)}, u32[]{:S(2)}) collective-permute-start(bf16[1,1,8,2,8,128]{5,2,4,3,1,0:T(8,128)(2,1)S(1)} %get-tuple-element.105), channel_id=1, source_target_pairs={{0,16},{2,18},{4,20},{6,22},{8,24},{10,26},{12,28},{14,30},{16,0},... | collective-permute-start | bytes 98312 | tf_op jit(solution)/shard_map/ppermute | solution.py:121
  191.7 11.2 %collective-permute-start.8 = (bf16[1,1,8,2,8,128]{5,2,4,3,1,0:T(8,128)(2,1)S(1)}, bf16[1,1,8,2,8,128]{5,2,4,3,1,0:T(8,128)(2,1)S(1)}, u32[]{:S(2)}, u32[]{:S(2)}) collective-permute-start(bf16[1,1,8,2,8,128]{5,2,4,3,1,0:T(8,128)(2,1)S(1)} %get-tuple-element.104), channel_id=1, source_target_pairs={{0,18},{2,16},{4,22},{6,20},{8,26},{10,24},{12,30},{14,28},{16,2},... | collective-permute-start | bytes 98312 | tf_op jit(solution)/shard_map/ppermute | solution.py:121
  193.3 13.4 %collective-permute-start.9 = (bf16[1,1,8,2,8,128]{5,2,4,3,1,0:T(8,128)(2,1)S(1)}, bf16[1,1,8,2,8,128]{5,2,4,3,1,0:T(8,128)(2,1)S(1)}, u32[]{:S(2)}, u32[]{:S(2)}) collective-permute-start(bf16[1,1,8,2,8,128]{5,2,4,3,1,0:T(8,128)(2,1)S(1)} %get-tuple-element.103), channel_id=1, source_target_pairs={{0,20},{2,22},{4,16},{6,18},{8,28},{10,30},{12,24},{14,26},{16,4},... | collective-permute-start | bytes 98312 | tf_op jit(solution)/shard_map/ppermute | solution.py:121
  196.0 12.6 %collective-permute-start.10 = (bf16[1,1,8,2,8,128]{5,2,4,3,1,0:T(8,128)(2,1)S(1)}, bf16[1,1,8,2,8,128]{5,2,4,3,1,0:T(8,128)(2,1)S(1)}, u32[]{:S(2)}, u32[]{:S(2)}) collective-permute-start(bf16[1,1,8,2,8,128]{5,2,4,3,1,0:T(8,128)(2,1)S(1)} %get-tuple-element.102), channel_id=1, source_target_pairs={{0,22},{2,20},{4,18},{6,16},{8,30},{10,28},{12,26},{14,24},{16,6},... | collective-permute-start | bytes 98312 | tf_op jit(solution)/shard_map/ppermute | solution.py:121
  198.1 11.1 %collective-permute-start.11 = (bf16[1,1,8,2,8,128]{5,2,4,3,1,0:T(8,128)(2,1)S(1)}, bf16[1,1,8,2,8,128]{5,2,4,3,1,0:T(8,128)(2,1)S(1)}, u32[]{:S(2)}, u32[]{:S(2)}) collective-permute-start(bf16[1,1,8,2,8,128]{5,2,4,3,1,0:T(8,128)(2,1)S(1)} %get-tuple-element.101), channel_id=1, source_target_pairs={{0,24},{2,26},{4,28},{6,30},{8,16},{10,18},{12,20},{14,22},{16,8},... | collective-permute-start | bytes 98312 | tf_op jit(solution)/shard_map/ppermute | solution.py:121
  200.8 9.1 %collective-permute-start.12 = (bf16[1,1,8,2,8,128]{5,2,4,3,1,0:T(8,128)(2,1)S(1)}, bf16[1,1,8,2,8,128]{5,2,4,3,1,0:T(8,128)(2,1)S(1)}, u32[]{:S(2)}, u32[]{:S(2)}) collective-permute-start(bf16[1,1,8,2,8,128]{5,2,4,3,1,0:T(8,128)(2,1)S(1)} %get-tuple-element.100), channel_id=1, source_target_pairs={{0,26},{2,24},{4,30},{6,28},{8,18},{10,16},{12,22},{14,20},{16,10}... | collective-permute-start | bytes 98312 | tf_op jit(solution)/shard_map/ppermute | solution.py:121
  202.9 7.6 %collective-permute-start.13 = (bf16[1,1,8,2,8,128]{5,2,4,3,1,0:T(8,128)(2,1)S(1)}, bf16[1,1,8,2,8,128]{5,2,4,3,1,0:T(8,128)(2,1)S(1)}, u32[]{:S(2)}, u32[]{:S(2)}) collective-permute-start(bf16[1,1,8,2,8,128]{5,2,4,3,1,0:T(8,128)(2,1)S(1)} %get-tuple-element.99), channel_id=1, source_target_pairs={{0,28},{2,30},{4,24},{6,26},{8,20},{10,22},{12,16},{14,18},{16,12}... | collective-permute-start | bytes 98312 | tf_op jit(solution)/shard_map/ppermute | solution.py:121
  206.7 6.1 %collective-permute-start.14 = (bf16[1,1,8,2,8,128]{5,2,4,3,1,0:T(8,128)(2,1)S(1)}, bf16[1,1,8,2,8,128]{5,2,4,3,1,0:T(8,128)(2,1)S(1)}, u32[]{:S(2)}, u32[]{:S(2)}) collective-permute-start(bf16[1,1,8,2,8,128]{5,2,4,3,1,0:T(8,128)(2,1)S(1)} %get-tuple-element.98), channel_id=1, source_target_pairs={{0,30},{2,28},{4,26},{6,24},{8,22},{10,20},{12,18},{14,16},{16,14}... | collective-permute-start | bytes 98312 | tf_op jit(solution)/shard_map/ppermute | solution.py:121
  213.4 12.1 %all-to-all-start.2 = ((bf16[16,1,8,2,8,128]{5,2,0,3,1,4:T(8,128)(2,1)}), bf16[16,1,8,2,8,128]{5,2,0,3,1,4:T(8,128)(2,1)S(1)}, u32[]{:S(2)}, u32[]{:S(2)}) async-start(bf16[16,1,8,2,8,128]{5,2,0,3,1,4:T(8,128)(2,1)} %copy_dynamic-update-slice_fusion), calls=%async_computation.2 | async-start | bytes 1048576 | tf_op jit(solution)/shard_map/all_to_all | solution.py:127
